TPU v7x, 256 devices: a whole 4x4x8 slice. The times are simulated.
256 devices in a mesh: section: 32 (over x_lo, z, core), expert: 8 (over x_hi, y).
Axes of the slice: x: 4 (x_hi: 2, x_lo: 2; x = x_hi * 2 + x_lo), y: 4, z: 8, core: 2. Of those that a mesh axis runs over, the one named last changes fastest.
Arguments:
- tokens: bfloat16 [2048, 3072], P(('section', 'expert')), may hold values from -6 to 6
- upstream: bfloat16 [2048, 3072], P(('section', 'expert')), may hold values from -2 to 2
- route_ids: int32 [2048, 2], P(('section', 'expert')), may hold values from 0 to 7, all different within a row; in each aligned block of 8 rows (0 to 7, 8 to 15, ...) at most 4 rows name the same one
- route_gates: bfloat16 [2048, 2], P(('section', 'expert')), may hold values from 0.099609375 to 0.8984375
- w_gate: bfloat16 [8, 3072, 8192], P('expert', None, 'section'), may hold values from -0.109375 to 0.109375
- w_up: bfloat16 [8, 3072, 8192], P('expert', None, 'section'), may hold values from -0.109375 to 0.109375
- w_down: bfloat16 [8, 8192, 3072], P('expert', 'section'), may hold values from -0.0625 to 0.0625
Outputs:
- grad_tokens: bfloat16 [2048, 3072], P(('section', 'expert'))
- grad_gates: float32 [2048, 2], P(('section', 'expert'))
- grad_w_gate: bfloat16 [8, 3072, 8192], P('expert', None, 'section')
- grad_w_up: bfloat16 [8, 3072, 8192], P('expert', None, 'section')
- grad_w_down: bfloat16 [8, 8192, 3072], P('expert', 'section')
Inputs may be any that keep to these rules, and one draw needn't show every extreme that they name: `route_ids`: the two experts of a token differ. Among the 16 choices of the tokens of one device, each expert is named at most 4 times, and in some device's tokens some expert is named exactly 4 times.
All inputs are finite; a program needn't handle non-finite values.
Results may differ from a plain program's by a relative error of at most 0.0058.
Values may be sent and summed in bfloat16 or wider, within the bound.
A program may use at most 128 MiB of HBM per device.

v0:
```python
import jax
import jax.numpy as jnp
from jax import lax
from jax.sharding import PartitionSpec as P


def slot_matrix(route_ids, experts, capacity):
    flattened = route_ids.reshape(-1)
    onehot = (flattened[:, None] == jnp.arange(experts, dtype=jnp.int32)[None, :]).astype(jnp.int32)
    before = jnp.cumsum(onehot, axis=0) - onehot
    position = jnp.sum(before * onehot, axis=1)
    target = flattened * capacity + position
    columns = jnp.arange(experts * capacity, dtype=jnp.int32)
    return target[:, None] == columns[None, :]


def contract_last(left, right):
    return lax.dot_general(
        left, right, (((1,), (1,)), ((), ())), preferred_element_type=jnp.float32
    )


def contract_first(left, right):
    return lax.dot_general(
        left, right, (((0,), (0,)), ((), ())), preferred_element_type=jnp.float32
    )


def local(tokens, upstream, route_ids, route_gates, w_gate, w_up, w_down):
    experts = lax.axis_size("expert")
    tok_count, features = tokens.shape
    capacity = min(tok_count, max(2, 4 * tok_count // experts))
    chosen_slots = slot_matrix(route_ids, experts, capacity)
    placement = chosen_slots.astype(jnp.bfloat16)
    gates = route_gates.reshape(-1).astype(jnp.float32)
    tokens_twice = jnp.repeat(tokens, 2, axis=0)
    scaled = (gates[:, None] * jnp.repeat(upstream, 2, axis=0).astype(jnp.float32)).astype(
        jnp.bfloat16
    )
    send_x = contract_first(placement, tokens_twice).astype(jnp.bfloat16)
    send_u = contract_first(placement, scaled).astype(jnp.bfloat16)
    send = jnp.concatenate(
        [send_x.reshape(experts, capacity, features), send_u.reshape(experts, capacity, features)],
        axis=1,
    )
    recv = lax.all_to_all(send, "expert", split_axis=0, concat_axis=0, tiled=True)
    mine = jnp.stack([recv[:, :capacity], recv[:, capacity:]]).reshape(
        2, experts * capacity, features
    )
    every = lax.all_gather(mine, "section", axis=1, tiled=True)
    rows_x, rows_u = (every[0], every[1])
    gate_slab = w_gate[0]
    up_slab = w_up[0]
    down_slab = w_down[0]
    pre_gate = jnp.dot(rows_x, gate_slab, preferred_element_type=jnp.float32)
    pre_up = jnp.dot(rows_x, up_slab, preferred_element_type=jnp.float32)
    sigmoid_gate = jax.nn.sigmoid(pre_gate)
    active = pre_gate * sigmoid_gate
    hidden = (active * pre_up).astype(jnp.bfloat16)
    d_hidden = contract_last(rows_u, down_slab)
    d_gate = (d_hidden * pre_up * (sigmoid_gate * (1.0 + pre_gate * (1.0 - sigmoid_gate)))).astype(
        jnp.bfloat16
    )
    d_up = (d_hidden * active).astype(jnp.bfloat16)
    grad_down = contract_first(hidden, rows_u)
    grad_gate = contract_first(rows_x, d_gate)
    grad_up = contract_first(rows_x, d_up)
    input_part = contract_last(d_gate, gate_slab) + contract_last(d_up, up_slab)
    gate_part = hidden.astype(jnp.float32) * d_hidden
    units = gate_part.shape[1]
    gate_part = sum((gate_part[:, i : i + 128] for i in range(0, units, 128)))
    part = jnp.concatenate([input_part, gate_part], axis=1)
    part_mine = lax.psum_scatter(part, "section", scatter_dimension=0, tiled=True)
    back = lax.all_to_all(
        part_mine.reshape(experts, capacity, features + 128),
        "expert",
        split_axis=0,
        concat_axis=0,
        tiled=True,
    ).reshape(experts * capacity, features + 128)
    selector = chosen_slots.astype(jnp.float32)
    choice = jnp.dot(selector, back, precision=lax.Precision.HIGHEST)
    grad_tokens = jnp.sum(choice[:, :features].reshape(tok_count, 2, features), axis=1)
    grad_gates = (jnp.sum(choice[:, features:], axis=1) / gates).reshape(tok_count, 2)
    return (
        grad_tokens.astype(jnp.bfloat16),
        grad_gates,
        grad_gate.astype(jnp.bfloat16)[None],
        grad_up.astype(jnp.bfloat16)[None],
        grad_down.astype(jnp.bfloat16)[None],
    )


def solution(mesh):
    placed = (
        P(("section", "expert"), None),
        P(("section", "expert"), None),
        P(("section", "expert"), None),
        P(("section", "expert"), None),
        P("expert", None, "section"),
        P("expert", None, "section"),
        P("expert", "section", None),
    )
    return jax.shard_map(
        local,
        mesh=mesh,
        in_specs=placed,
        out_specs=(
            P(("section", "expert"), None),
            P(("section", "expert"), None),
            P("expert", None, "section"),
            P("expert", None, "section"),
            P("expert", "section", None),
        ),
        check_vma=False,
    )
```

profile of v0, /device:TPU:2, one launch (start us, length us, event | category | flops | bytes accessed | tf_op | source)
XLA Modules:
  0.0 304.9 jit_solution(16035402707329511470)
XLA Ops:
  7.2 0.0 copy-start
  7.2 0.0 all-gather.2.cloned.1.call-start
  7.2 0.9 copy.17
  8.1 0.1 reshape.64
  8.2 0.8 copy.16
  8.9 0.1 reshape.57
  9.0 0.1 fusion.21
  9.1 0.2 select_reduce_fusion
  9.3 0.9 broadcast_in_dim.19
  10.2 0.3 convolution_convert_fusion.1
  10.5 0.1 reshape.59
  10.6 0.9 broadcast_in_dim.20
  11.5 0.1 convert_element_type.63
  11.6 0.3 convolution_convert_fusion
  11.9 0.1 reshape.60
  12.0 0.2 pad_maximum_fusion.1
  12.2 16.0 %all_to_all.10 = bf16[8,8,3072]{2,1,0:T(8,128)(2,1)S(1)} all-to-all(bf16[8,8,3072]{2,1,0:T(8,128)(2,1)S(1)} %pad_maximum_fusion.1), channel_id=1, replica_groups=mesh['section'=32,'expert'=8] {'expert'}, dimensions={0} | all-to-all | bytes 786432 | tf_op jit(solution)/shard_map/all_to_all | solution.py:46
  28.3 0.1 fusion.25
  28.5 0.8 pad_maximum_fusion.2
  29.3 0.0 all-gather.2.cloned.1.call-update
  29.3 0.0 copy-start.2
  29.3 0.0 reduce-scatter.2.cloned.1.call-start
  29.4 79.5 %all-gather.2.cloned.1.call-done = bf16[2,1024,3072]{2,1,0:T(8,128)(2,1)} async-done(((bf16[2,32,3072]{2,1,0:T(8,128)(2,1)}), bf16[2,1024,3072]{2,1,0:T(8,128)(2,1)}) %all-gather.2.cloned.1.call-update) | async-done | bytes 12582928 | tf_op jit(solution)/shard_map/all_gather | solution.py:50
  108.8 0.0 copy-done
  108.8 0.0 copy-start.5
  108.8 4.8 %fusion.4 = f32[1024,256]{0,1:T(8,128)S(1)} fusion(bf16[2,1024,3072]{2,1,0:T(8,128)(2,1)} %all-gather.2.cloned.1.call-done, bf16[1,3072,256]{2,1,0:T(8,128)(2,1)S(1)} %copy-done), kind=kOutput, calls=%fused_computation.8 | convolution fusion | flops 1610612736 | bytes 8912896 | tf_op jit(solution)/shard_map/dot_general | solution.py:55
  113.6 0.0 copy-done.2
  113.6 1.6 copy-done.5
  115.2 0.0 copy-start.6
  115.2 1.9 fusion.5
  117.1 0.0 copy-done.6
  117.1 3.2 %convert_multiply_fusion = (f32[1024,256]{0,1:T(8,128)S(1)}, bf16[1024,256]{0,1:T(8,128)(2,1)}, bf16[1024,256]{0,1:T(8,128)(2,1)}, bf16[1024,256]{0,1:T(8,128)(2,1)S(1)}) fusion(f32[1024,256]{0,1:T(8,128)S(1)} %fusion.5, f32[1024,256]{0,1:T(8,128)S(1)} %fusion.4, bf16[1,256,3072]{2,1,0:T(8,128)(2,1)S(1)} %copy-done.6, bf16[2,1024,3072]{2,1,0:T(8,128)(2,1)S(1)} %copy-done.5), kind=kOutput, calls=%fused_computation.24 | convolution fusion | flops 1615069184 | bytes 12582912 | tf_op jit(solution)/shard_map/dot_general | solution.py:18
  120.3 0.1 slice_add_fusion
  120.3 0.2 copy.18
  120.5 0.0 copy-start.3
  120.6 3.0 fusion.12
  123.6 0.0 copy-done.3
  123.6 6.5 %convolution_add_fusion = f32[1024,3072]{1,0:T(8,128)} fusion(f32[1024,3072]{1,0:T(8,128)S(1)} %fusion.12, bf16[1024,256]{0,1:T(8,128)(2,1)S(1)} %get-tuple-element.18, bf16[1,3072,256]{2,1,0:T(8,128)(2,1)S(1)} %copy-done.3), kind=kOutput, calls=%fused_computation.1 | convolution fusion | flops 1613758464 | bytes 27262976 | tf_op jit(solution)/shard_map/dot_general | solution.py:18
  130.1 10.3 %pad_maximum_fusion = f32[1024,3200]{1,0:T(8,128)} fusion(f32[1024,128]{1,0:T(8,128)S(1)} %copy.18, f32[1024,3072]{1,0:T(8,128)} %convolution_add_fusion), kind=kLoop, calls=%fused_computation | loop fusion | flops 3276800 | bytes 26214400 | tf_op jit(solution)/shard_map/concatenate | solution.py:72
  140.4 0.0 copy-start.4
  140.4 0.0 reduce-scatter.2.cloned.1.call-update
  140.4 1.0 copy-done.4
  141.4 6.0 %fusion.11 = bf16[1,3072,256]{2,1,0:T(8,128)(2,1)} fusion(bf16[1024,256]{0,1:T(8,128)(2,1)S(1)} %copy-done.4, bf16[2,1024,3072]{2,1,0:T(8,128)(2,1)} %all-gather.2.cloned.1.call-done), kind=kOutput, calls=%fused_computation.15 | convolution fusion | flops 1611399168 | bytes 8388608 | tf_op jit(solution)/shard_map/dot_general | solution.py:24
  147.5 0.0 copy-start.7
  147.5 5.9 %fusion.10 = bf16[1,3072,256]{2,1,0:T(8,128)(2,1)} fusion(bf16[1024,256]{0,1:T(8,128)(2,1)S(1)} %get-tuple-element.18, bf16[2,1024,3072]{2,1,0:T(8,128)(2,1)} %all-gather.2.cloned.1.call-done), kind=kOutput, calls=%fused_computation.14 | convolution fusion | flops 1611399168 | bytes 8388608 | tf_op jit(solution)/shard_map/dot_general | solution.py:24
  153.4 125.1 %reduce-scatter.2.cloned.1.call-done = f32[32,3200]{1,0:T(8,128)} async-done(((f32[1024,3200]{1,0:T(8,128)}), f32[32,3200]{1,0:T(8,128)}) %reduce-scatter.2.cloned.1.call-update) | async-done | bytes 409616 | tf_op jit(solution)/shard_map/reduce_scatter | solution.py:73
  278.5 1.9 reshape.61
  280.3 6.1 %all-to-all-start.1 = ((f32[8,4,3200]{2,1,0:T(4,128)}), f32[8,4,3200]{2,1,0:T(4,128)S(1)}, u32[]{:S(2)}, u32[]{:S(2)}) async-start(f32[8,4,3200]{2,1,0:T(4,128)} %reshape.61), calls=%async_computation.2 | async-start | bytes 819200 | tf_op jit(solution)/shard_map/all_to_all | solution.py:74
  286.5 0.0 copy-start.1
  286.5 0.0 copy-done.7
  286.5 5.9 %fusion.9 = bf16[1,256,3072]{2,1,0:T(8,128)(2,1)} fusion(bf16[1024,256]{0,1:T(8,128)(2,1)S(1)} %copy-done.7, bf16[2,1024,3072]{2,1,0:T(8,128)(2,1)} %all-gather.2.cloned.1.call-done), kind=kOutput, calls=%fused_computation.13 | convolution fusion | flops 1611399168 | bytes 8388608 | tf_op jit(solution)/shard_map/dot_general | solution.py:24
  292.4 3.4 %all-to-all-done.1 = f32[8,4,3200]{2,1,0:T(4,128)S(1)} async-done(((f32[8,4,3200]{2,1,0:T(4,128)}), f32[8,4,3200]{2,1,0:T(4,128)S(1)}, u32[]{:S(2)}, u32[]{:S(2)}) %all-to-all-start.1) | async-done | bytes 409632 | tf_op jit(solution)/shard_map/all_to_all | solution.py:74
  295.8 0.1 reshape.62
  296.0 0.3 fusion.20
  296.2 0.1 slice_reduce_fusion
  296.4 0.1 reshape.63
  296.5 0.1 reduce_sum.32
  296.6 0.6 copy.19
  297.2 0.9 reduce_sum.30
  298.1 0.0 copy-done.1
  (7 shorter events, 0.2 us)
Async XLA Ops:
  7.2 101.7 %copy-start = (bf16[1,3072,256]{2,1,0:T(8,128)(2,1)S(1)}, bf16[1,3072,256]{2,1,0:T(8,128)(2,1)}, u32[]{:S(2)}) copy-start(bf16[1,3072,256]{2,1,0:T(8,128)(2,1)} %param.11) | copy-start | bytes 4718596
  7.2 101.7 %all-gather.2.cloned.1.call-start = ((), (), s32[]{:S(2)}) async-start(), calls=%async_computation.3 | async-start | bytes 12976128 | tf_op jit(solution)/shard_map/all_gather | solution.py:50
  29.3 84.3 %copy-start.2 = (bf16[1,3072,256]{2,1,0:T(8,128)(2,1)S(1)}, bf16[1,3072,256]{2,1,0:T(8,128)(2,1)}, u32[]{:S(2)}) copy-start(bf16[1,3072,256]{2,1,0:T(8,128)(2,1)} %param.12) | copy-start | bytes 4718596
  29.3 249.2 %reduce-scatter.2.cloned.1.call-start = ((), (), s32[]{:S(2)}) async-start(), calls=%async_computation.4 | async-start | bytes 13516800 | tf_op jit(solution)/shard_map/reduce_scatter | solution.py:73
  108.8 6.4 %copy-start.5 = (bf16[2,1024,3072]{2,1,0:T(8,128)(2,1)S(1)}, bf16[2,1024,3072]{2,1,0:T(8,128)(2,1)}, u32[]{:S(2)}) copy-start(bf16[2,1024,3072]{2,1,0:T(8,128)(2,1)} %all-gather.2.cloned.1.call-done) | copy-start | bytes 37748740
  115.2 1.9 copy-start.6
  120.5 3.0 copy-start.3
  140.4 1.0 copy-start.4
  147.5 139.0 %copy-start.7 = (bf16[1024,256]{0,1:T(8,128)(2,1)S(1)}, bf16[1024,256]{0,1:T(8,128)(2,1)}, u32[]{:S(2)}) copy-start(bf16[1024,256]{0,1:T(8,128)(2,1)} %get-tuple-element.16) | copy-start | bytes 1572868
  280.3 15.5 %all-to-all-start.1 = ((f32[8,4,3200]{2,1,0:T(4,128)}), f32[8,4,3200]{2,1,0:T(4,128)S(1)}, u32[]{:S(2)}, u32[]{:S(2)}) async-start(f32[8,4,3200]{2,1,0:T(4,128)} %reshape.61), calls=%async_computation.2 | async-start | bytes 819200 | tf_op jit(solution)/shard_map/all_to_all | solution.py:74
  286.5 11.6 %copy-start.1 = (bf16[1,3072,256]{2,1,0:T(8,128)(2,1)S(1)}, bf16[1,3072,256]{2,1,0:T(8,128)(2,1)}, u32[]{:S(2)}) copy-start(bf16[1,3072,256]{2,1,0:T(8,128)(2,1)} %param.11) | copy-start | bytes 4718596
Sparse Core Ops, SparseCore 0:
  29.4 79.3 all-gather.1
  140.5 137.8 reduce-scatter.1
where the time goes:
time: 305 us
  waiting for transfers between devices  208 us (68%)
  matrix products  38 us (12%)
  blocking collectives  16 us (5%)
  between operations  14.2 us (5%)
  other arithmetic  12.6 us (4%)
  local copies, waits for them, and re-layouts  9.78 us (3%)
  starting transfers between devices  6.22 us (2%)
    reduce_scatter x1, waiting for transfers between devices, local(): lax.psum_scatter(part, 'section', scatter_dimension=0, tiled=True)  125 us
    all_gather x1, waiting for transfers between devices, local(): every = lax.all_gather(mine, 'section', axis=1, tiled=True)  79.5 us
    dot_general x5, matrix products, contract_first(): lax.dot_general(left, right, (((0,), (0,)), ((), ())), preferred_element_...  18.4 us
    all_to_all x1, blocking collectives, local(): lax.all_to_all(send, 'expert', split_axis=0, concat_axis=0, tiled=True)  16 us
    dot_general x3, matrix products, contract_last(): lax.dot_general(left, right, (((1,), (1,)), ((), ())), preferred_element_...  12.7 us
    concatenate x1, other arithmetic, local(): part = jnp.concatenate([input_part, gate_part], axis=1)  10.3 us
    all_to_all x1, starting transfers between devices, local(): lax.all_to_all(part_mine.reshape(experts, capacity, features + 128), 'exp...  6.14 us
  transfers between devices with their start and end apart: 3, of which 3 were waited for; matrix products, arithmetic and copies ran while one was open for 6% of the time, Pallas kernels for 0%

commit v1 on v0

--- a/solution.py
+++ b/solution.py
@@ -47,7 +47,9 @@
     mine = jnp.stack([recv[:, :capacity], recv[:, capacity:]]).reshape(
         2, experts * capacity, features
     )
-    every = lax.all_gather(mine, "section", axis=1, tiled=True)
+    every = jnp.concatenate(
+        lax.all_to_all(jnp.stack([mine] * lax.axis_size("section")), "section", 0, 0), axis=1
+    )
     rows_x, rows_u = (every[0], every[1])
     gate_slab = w_gate[0]
     up_slab = w_up[0]

time: 305 us -> 510 us (1.67)
  blocking collectives: 16 us -> 301 us
  waiting for transfers between devices: 208 us -> 123 us
  local copies, waits for them, and re-layouts: 9.78 us -> 18.4 us
    all_to_all x0 -> x1, blocking collectives: none -> 285 us  [local(): lax.all_to_all(jnp.stack([mine] * lax.axis_size('section')), 'section', 0...]
    all_gather x1 -> x0, waiting for transfers between devices: 79.5 us -> none  [local(): every = lax.all_gather(mine, 'section', axis=1, tiled=True)]
    another operation x0 -> x1, local copies, waits for them, and re-layouts: none -> 6.15 us  [local(): jnp.stack([mine] * lax.axis_size('section'))]
  transfers between devices with their start and end apart: 3 -> 2, of which waited for: 3 -> 2; matrix products, arithmetic and copies ran while one was open for 6% -> 3% of each run, Pallas kernels for 0% -> 0%
where the time goes in v1:
time: 510 us
  blocking collectives  301 us (59%)
  waiting for transfers between devices  123 us (24%)
  matrix products  35 us (7%)
  local copies, waits for them, and re-layouts  18.4 us (4%)
  between operations  14.3 us (3%)
  other arithmetic  11.9 us (2%)
  starting transfers between devices  6.19 us (1%)
    all_to_all x1, blocking collectives, local(): lax.all_to_all(jnp.stack([mine] * lax.axis_size('section')), 'section', 0...  285 us
    reduce_scatter x1, waiting for transfers between devices, local(): lax.psum_scatter(part, 'section', scatter_dimension=0, tiled=True)  120 us
    dot_general x5, matrix products, contract_first(): lax.dot_general(left, right, (((0,), (0,)), ((), ())), preferred_element_...  18.4 us
    all_to_all x1, blocking collectives, local(): lax.all_to_all(send, 'expert', split_axis=0, concat_axis=0, tiled=True)  16 us
    dot_general x3, matrix products, contract_last(): lax.dot_general(left, right, (((1,), (1,)), ((), ())), preferred_element_...  12.6 us
    concatenate x1, other arithmetic, local(): part = jnp.concatenate([input_part, gate_part], axis=1)  10.3 us
  transfers between devices with their start and end apart: 2, of which 2 were waited for; matrix products, arithmetic and copies ran while one was open for 3% of the time, Pallas kernels for 0%

profile of v1, /device:TPU:2, one launch (start us, length us, event | category | flops | bytes accessed | tf_op | source)
XLA Modules:
  0.0 509.8 jit_solution(6853871788540877860)
XLA Ops:
  7.2 0.0 copy-start
  7.2 0.0 reduce-scatter.2.cloned.1.call-start
  7.2 0.9 copy.17
  8.1 0.1 reshape.73
  8.2 0.8 copy.16
  8.9 0.1 reshape.65
  9.0 0.1 fusion.15
  9.1 0.2 select_reduce_fusion
  9.3 0.9 broadcast_in_dim.19
  10.2 0.3 convolution_convert_fusion.4
  10.5 0.1 reshape.67
  10.6 0.9 broadcast_in_dim.20
  11.5 0.1 convert_element_type.63
  11.6 0.3 convolution_convert_fusion.3
  11.9 0.1 reshape.68
  12.0 0.2 pad_maximum_fusion.1
  12.2 16.0 %all_to_all.15 = bf16[8,8,3072]{2,1,0:T(8,128)(2,1)S(1)} all-to-all(bf16[8,8,3072]{2,1,0:T(8,128)(2,1)S(1)} %pad_maximum_fusion.1), channel_id=1, replica_groups=mesh['section'=32,'expert'=8] {'expert'}, dimensions={0} | all-to-all | bytes 786432 | tf_op jit(solution)/shard_map/all_to_all | solution.py:46
  28.3 0.1 fusion.20
  28.5 6.2 %stack.15 = bf16[32,2,32,3072]{3,2,1,0:T(8,128)(2,1)} broadcast(bf16[2,32,3072]{2,1,0:T(8,128)(2,1)S(1)} %maximum_bitcast_fusion), dimensions={1,2,3} | broadcast | bytes 12976128 | tf_op jit(solution)/shard_map/stack | solution.py:51
  34.7 284.6 %all_to_all.16 = bf16[32,2,32,3072]{3,2,1,0:T(8,128)(2,1)S(1)} all-to-all(bf16[32,2,32,3072]{3,2,1,0:T(8,128)(2,1)} %stack.15), channel_id=1, replica_groups=mesh['section'=32,'expert'=8] {'section'}, dimensions={0} | all-to-all | bytes 25165824 | tf_op jit(solution)/shard_map/all_to_all | solution.py:51
  319.3 2.6 fusion.19
  322.0 0.0 copy-start.3
  322.0 0.0 copy-start.2
  322.0 0.0 copy-done
  322.0 0.0 copy-start.4
  322.0 1.9 fusion.5
  323.9 0.8 copy-done.3
  324.7 0.0 copy-done.4
  324.7 0.0 copy-start.7
  324.7 1.9 fusion.8
  326.6 0.6 copy-done.2
  327.1 0.1 copy-done.7
  327.2 3.2 convert_multiply_fusion
  330.4 0.1 slice_add_fusion
  330.4 0.2 copy.18
  330.6 0.0 copy-start.5
  330.6 3.0 fusion.3
  333.7 0.0 copy-done.5
  333.7 6.4 %convolution_add_fusion = f32[1024,3072]{1,0:T(8,128)} fusion(f32[1024,3072]{1,0:T(8,128)S(1)} %fusion.3, bf16[1024,256]{0,1:T(8,128)(2,1)S(1)} %get-tuple-element.20, bf16[1,3072,256]{2,1,0:T(8,128)(2,1)S(1)} %copy-done.5), kind=kOutput, calls=%fused_computation.1 | convolution fusion | flops 1613758464 | bytes 27262976 | tf_op jit(solution)/shard_map/dot_general | solution.py:18
  340.1 10.3 %pad_maximum_fusion = f32[1024,3200]{1,0:T(8,128)} fusion(f32[1024,128]{1,0:T(8,128)S(1)} %copy.18, f32[1024,3072]{1,0:T(8,128)} %convolution_add_fusion), kind=kLoop, calls=%fused_computation | loop fusion | flops 3276800 | bytes 26214400 | tf_op jit(solution)/shard_map/concatenate | solution.py:74
  350.4 0.0 copy-start.6
  350.4 0.0 reduce-scatter.2.cloned.1.call-update
  350.4 1.0 copy-done.6
  351.4 6.1 %fusion = bf16[1,3072,256]{2,1,0:T(8,128)(2,1)} fusion(bf16[1024,3072]{1,0:T(8,128)(2,1)} %bitcast.44, bf16[1024,256]{0,1:T(8,128)(2,1)S(1)} %copy-done.6), kind=kOutput, calls=%fused_computation.5 | convolution fusion | flops 1611399168 | bytes 8388608 | tf_op jit(solution)/shard_map/dot_general | solution.py:24
  357.5 0.0 copy-start.8
  357.5 5.9 %fusion.1 = bf16[1,3072,256]{2,1,0:T(8,128)(2,1)} fusion(bf16[1024,3072]{1,0:T(8,128)(2,1)} %bitcast.45, bf16[1024,256]{0,1:T(8,128)(2,1)S(1)} %get-tuple-element.20), kind=kOutput, calls=%fused_computation.6 | convolution fusion | flops 1611399168 | bytes 8388608 | tf_op jit(solution)/shard_map/dot_general | solution.py:24
  363.4 120.0 %reduce-scatter.2.cloned.1.call-done = f32[32,3200]{1,0:T(8,128)} async-done(((f32[1024,3200]{1,0:T(8,128)}), f32[32,3200]{1,0:T(8,128)}) %reduce-scatter.2.cloned.1.call-update) | async-done | bytes 409616 | tf_op jit(solution)/shard_map/reduce_scatter | solution.py:75
  483.4 1.9 reshape.70
  485.2 6.1 %all-to-all-start.2 = ((f32[8,4,3200]{2,1,0:T(4,128)}), f32[8,4,3200]{2,1,0:T(4,128)S(1)}, u32[]{:S(2)}, u32[]{:S(2)}) async-start(f32[8,4,3200]{2,1,0:T(4,128)} %reshape.70), calls=%async_computation.3 | async-start | bytes 819200 | tf_op jit(solution)/shard_map/all_to_all | solution.py:76
  491.4 0.0 copy-start.1
  491.4 0.0 copy-done.8
  491.4 5.8 %fusion.2 = bf16[1,256,3072]{2,1,0:T(8,128)(2,1)} fusion(bf16[1024,256]{0,1:T(8,128)(2,1)S(1)} %copy-done.8, bf16[1024,3072]{1,0:T(8,128)(2,1)} %bitcast.41), kind=kOutput, calls=%fused_computation.7 | convolution fusion | flops 1611399168 | bytes 8388608 | tf_op jit(solution)/shard_map/dot_general | solution.py:24
  497.2 3.5 all-to-all-done.2
  500.7 0.1 reshape.71
  500.9 0.3 fusion.14
  501.1 0.1 slice_reduce_fusion
  501.3 0.1 reshape.72
  501.4 0.1 reduce_sum.32
  501.5 0.6 copy.19
  502.1 0.9 reduce_sum.30
  503.0 0.0 copy-done.1
  (8 shorter events, 0.2 us)
Async XLA Ops:
  7.2 314.8 %copy-start = (bf16[1,3072,256]{2,1,0:T(8,128)(2,1)S(1)}, bf16[1,3072,256]{2,1,0:T(8,128)(2,1)}, u32[]{:S(2)}) copy-start(bf16[1,3072,256]{2,1,0:T(8,128)(2,1)} %param.11) | copy-start | bytes 4718596
  7.2 476.2 %reduce-scatter.2.cloned.1.call-start = ((), (), s32[]{:S(2)}) async-start(), calls=%async_computation.4 | async-start | bytes 13516800 | tf_op jit(solution)/shard_map/reduce_scatter | solution.py:75
  322.0 2.7 copy-start.3
  322.0 5.1 %copy-start.2 = (bf16[1,32,32,3072]{3,2,0,1:T(8,128)(2,1)}, bf16[1,32,32,3072]{3,2,0,1:T(8,128)(2,1)S(1)}, u32[]{:S(2)}) copy-start(bf16[1,32,32,3072]{3,2,0,1:T(8,128)(2,1)S(1)} %get-tuple-element.18) | copy-start | bytes 18874372
  322.0 2.7 copy-start.4
  324.7 2.5 copy-start.7
  330.6 3.0 copy-start.5
  350.4 1.0 copy-start.6
  357.5 133.9 %copy-start.8 = (bf16[1024,256]{0,1:T(8,128)(2,1)S(1)}, bf16[1024,256]{0,1:T(8,128)(2,1)}, u32[]{:S(2)}) copy-start(bf16[1024,256]{0,1:T(8,128)(2,1)} %get-tuple-element.16) | copy-start | bytes 1572868
  485.2 15.5 %all-to-all-start.2 = ((f32[8,4,3200]{2,1,0:T(4,128)}), f32[8,4,3200]{2,1,0:T(4,128)S(1)}, u32[]{:S(2)}, u32[]{:S(2)}) async-start(f32[8,4,3200]{2,1,0:T(4,128)} %reshape.70), calls=%async_computation.3 | async-start | bytes 819200 | tf_op jit(solution)/shard_map/all_to_all | solution.py:76
  491.4 11.6 %copy-start.1 = (bf16[1,3072,256]{2,1,0:T(8,128)(2,1)S(1)}, bf16[1,3072,256]{2,1,0:T(8,128)(2,1)}, u32[]{:S(2)}) copy-start(bf16[1,3072,256]{2,1,0:T(8,128)(2,1)} %param.11) | copy-start | bytes 4718596
Sparse Core Ops, SparseCore 0:
  350.5 132.8 reduce-scatter.1
